TPU v7x, 256 devices: a whole 4x4x8 slice. The times are simulated.
256 devices in a mesh: head: 4 (over x_hi, core), vis: 32 (over y, z), sec: 2 (over x_lo).
Axes of the slice: x: 4 (x_hi: 2, x_lo: 2; x = x_hi * 2 + x_lo), y: 4, z: 8, core: 2. Of those that a mesh axis runs over, the one named last changes fastest.
Arguments:
- text_states: bfloat16 [256, 8192], P(None, 'vis'), may hold values from -6 to 6
- w_query: bfloat16 [8192, 8192], P('vis', ('head', 'sec')), may hold values from -0.0625 to 0.0625
- w_out: bfloat16 [8192, 8192], P(('head', 'sec'), 'vis'), may hold values from -0.25 to 0.25
- visual_keys: bfloat16 [262144, 1024], P('vis', ('head', 'sec')), may hold values from -120 to 120
- visual_values: bfloat16 [262144, 1024], P('vis', ('head', 'sec')), may hold values from -6 to 6
- block_list: int32 [2, 32, 32], P(None, 'vis'), may hold values from -1 to 63, as said below
Outputs:
- projected: bfloat16 [256, 8192], P(('head', 'sec'), 'vis')
Inputs may be any that keep to these rules, and one draw needn't show every extreme that they name: `block_list`: for each query block and shard, the entries that are not -1 are distinct and come first; each query block selects exactly 512 key blocks in all (a quarter), between 0 and 32 from one shard, and exactly 32 from some shard.
All inputs are finite; a program needn't handle non-finite values.
Results may differ from a plain program's by a relative error of at most 0.012.
Values may be sent and summed in bfloat16 or wider, within the bound.
No kernel may reach another device: no remote copies, remote signals or barrier semaphores. Data moves between devices by JAX's collectives and lax.ppermute only.
A program may use at most 192 MiB of HBM per device.

v0:
```python
import functools

import jax
import jax.numpy as jnp
import numpy as np
from jax import lax
from jax.experimental import pallas as pl
from jax.experimental.pallas import tpu as pltpu
from jax.sharding import Mesh, PartitionSpec as P

HEAD_SIZE = 128
BLOCK_TOKENS = 128
BIG, MID, SMALL, TILE = 8, 4, 2, 256
NEG_FILL = -1e30
EXP2_SCALE = float(np.log2(np.e) / np.sqrt(HEAD_SIZE))


def split3(x):
    hi = x.astype(jnp.bfloat16).astype(jnp.float32)
    rest = x - hi
    mid = rest.astype(jnp.bfloat16).astype(jnp.float32)
    return hi, mid, rest - mid


def pack_stats(top, total, heads):
    lane = lax.broadcasted_iota(jnp.int32, top[0].shape, 1)
    both = jnp.zeros(top[0].shape, jnp.float32)
    for h in range(heads):
        both = jnp.where(lane == h, top[h], both)
        both = jnp.where(lane == 3 * heads + h, total[h], both)
    hi, mid, low = split3(both)
    packed = hi + pltpu.roll(mid, heads, 1) + pltpu.roll(low, 2 * heads, 1)
    return packed.astype(jnp.bfloat16)


def attention_kernel(heads, ids_ref, q_ref, k_ref, v_ref, out_ref, q_rows, top_ref, acc_ref):
    query_blocks = q_ref.shape[0] // BLOCK_TOKENS
    slots = ids_ref.shape[1]
    rows = heads * BLOCK_TOKENS

    def query_block(b, carry):
        tokens = pl.ds(pl.multiple_of(b * BLOCK_TOKENS, BLOCK_TOKENS), BLOCK_TOKENS)
        for h in range(heads):
            hc = slice(h * 128, (h + 1) * 128)
            q_rows[hc, :] = q_ref[tokens, hc]
        top_ref[...] = jnp.full(top_ref.shape, NEG_FILL, jnp.float32)
        acc_ref[...] = jnp.zeros(acc_ref.shape, jnp.float32)
        count = lax.fori_loop(
            0, slots, lambda j, c: c + (ids_ref[b, j] >= 0).astype(jnp.int32), jnp.int32(0)
        )

        def blocks(first, size, masked):
            ks, vs = [], []
            for i in range(size):
                j = first + i
                block = ids_ref[b, jnp.minimum(j, count - 1) if masked else j]
                start = pl.multiple_of(block * BLOCK_TOKENS, BLOCK_TOKENS)
                ks.append(k_ref[pl.ds(start, BLOCK_TOKENS), :])
                value = v_ref[pl.ds(start, BLOCK_TOKENS), :]
                flag = jnp.full((BLOCK_TOKENS, 128), 1.0, jnp.bfloat16)
                if masked:
                    live = jnp.where(j < count, 1.0, 0.0).astype(jnp.float32)
                    value = (value.astype(jnp.float32) * live).astype(jnp.bfloat16)
                    flag = (jnp.full((BLOCK_TOKENS, 128), 1.0, jnp.float32) * live).astype(jnp.bfloat16)
                vs.append(jnp.concatenate([value, flag], axis=1))
            kc = jnp.concatenate(ks, axis=0)
            vc = jnp.concatenate(vs, axis=0)
            score = lambda r: lax.dot_general(
                q_rows[pl.ds(r * TILE, TILE), :],
                kc,
                (((1,), (1,)), ((), ())),
                preferred_element_type=jnp.float32,
            )
            tiles = rows // TILE
            ahead = score(0)
            for r in range(tiles):
                rs = pl.ds(r * TILE, TILE)
                s = ahead
                if r + 1 < tiles:
                    ahead = score(r + 1)
                old = top_ref[rs, :]
                new = jnp.maximum(old, jnp.max(s, axis=1, keepdims=True))
                alpha = jnp.exp2((old - new) * EXP2_SCALE)
                wide = jnp.concatenate([new] * size, axis=1)
                p = jnp.exp2((s - wide) * EXP2_SCALE).astype(jnp.bfloat16)
                pv = jnp.dot(p, vc, preferred_element_type=jnp.float32)
                acc_ref[rs, :] = acc_ref[rs, :] * jnp.concatenate([alpha, alpha], axis=1) + pv
                top_ref[rs, :] = new

        full = lax.shift_right_logical(count, 3)
        left = count - full * BIG
        some = lax.shift_right_logical(left, 2)
        rest = left - some * MID

        def big(c, carry):
            blocks(c * BIG, BIG, False)
            return carry

        def mid(c, carry):
            blocks(full * BIG, MID, False)
            return carry

        def small(c, carry):
            blocks(full * BIG + some * MID + c * SMALL, SMALL, True)
            return carry

        lax.fori_loop(0, full, big, 0)
        lax.fori_loop(0, some, mid, 0)
        lax.fori_loop(0, lax.shift_right_logical(rest + 1, 1), small, 0)
        tops, totals = [], []
        for h in range(heads):
            hc = slice(h * 128, (h + 1) * 128)
            out_ref[tokens, hc] = acc_ref[hc, :128].astype(jnp.bfloat16)
            tops.append(top_ref[hc, :])
            totals.append(acc_ref[hc, 128:])
        out_ref[tokens, heads * 128 :] = pack_stats(tops, totals, heads)
        return carry

    lax.fori_loop(0, query_blocks, query_block, 0)


def attention(ids, q, k, v):
    heads = q.shape[1] // HEAD_SIZE
    rows = heads * BLOCK_TOKENS
    vmem = pl.BlockSpec(memory_space=pltpu.VMEM)
    k = pltpu.with_memory_space_constraint(k, pltpu.VMEM)
    v = pltpu.with_memory_space_constraint(v, pltpu.VMEM)
    return pl.pallas_call(
        functools.partial(attention_kernel, heads),
        out_shape=jax.ShapeDtypeStruct((q.shape[0], q.shape[1] + 128), jnp.bfloat16),
        in_specs=[pl.BlockSpec(memory_space=pltpu.SMEM), vmem, vmem, vmem],
        out_specs=vmem,
        scratch_shapes=[
            pltpu.VMEM((rows, 128), jnp.bfloat16),
            pltpu.VMEM((rows, 128), jnp.float32),
            pltpu.VMEM((rows, 256), jnp.float32),
        ],
        compiler_params=pltpu.CompilerParams(vmem_limit_bytes=24 * 2**20),
        name="attend",
    )(ids, q, k, v)


def merge_kernel(heads, parts_ref, out_ref):
    sources, copies = parts_ref.shape[0], out_ref.shape[0]
    wide = heads * 128

    def gather3(stats, first):
        total = stats if first == 0 else pltpu.roll(stats, 128 - first * heads, 1)
        for i in (1, 2):
            total = total + pltpu.roll(stats, 128 - (first + i) * heads, 1)
        return total

    stats = [parts_ref[s, :, wide:].astype(jnp.float32) for s in range(sources)]
    tops = [gather3(x, 0) for x in stats]
    top = functools.reduce(jnp.maximum, tops)
    scales = [jnp.exp2((t - top) * EXP2_SCALE) for t in tops]
    total = functools.reduce(jnp.add, [gather3(x, 3) * scale for x, scale in zip(stats, scales)])
    for h in range(heads):
        hc = slice(h * 128, (h + 1) * 128)
        acc = jnp.zeros((parts_ref.shape[1], 128), jnp.float32)
        for s in range(sources):
            acc = acc + scales[s][:, h : h + 1] * parts_ref[s, :, hc].astype(jnp.float32)
        out = (acc / total[:, h : h + 1]).astype(jnp.bfloat16)
        for c in range(copies):
            out_ref[c, :, hc] = out


def merge(parts, copies):
    _, rows, width = parts.shape
    vmem = pl.BlockSpec(memory_space=pltpu.VMEM)
    return pl.pallas_call(
        functools.partial(merge_kernel, width // 128 - 1),
        out_shape=jax.ShapeDtypeStruct((copies, rows, width - 128), jnp.bfloat16),
        in_specs=[vmem],
        out_specs=vmem,
        compiler_params=pltpu.CompilerParams(vmem_limit_bytes=12 * 2**20),
        name="merge",
    )(parts)


def project_kernel(place_ref, attended_ref, *refs):
    w_refs, out_ref = refs[:-1], refs[-1]
    count = len(w_refs)
    groups, _, rows, _ = out_ref.shape
    attended = attended_ref[...]
    for k, w_ref in enumerate(w_refs):
        place = lax.rem(place_ref[0] + (count - k), count)
        out = jnp.dot(attended, w_ref[...], preferred_element_type=jnp.float32)
        out = out.astype(jnp.bfloat16)
        for g in range(groups):
            out_ref[g, place] = out[g * rows : (g + 1) * rows]


def project(attended, weights, groups, axis):
    count = len(weights)
    vmem = pl.BlockSpec(memory_space=pltpu.VMEM)
    place = jnp.reshape(lax.axis_index(axis), (1,)).astype(jnp.int32)
    rows, cols = attended.shape[0] // groups, weights[0].shape[1]
    return pl.pallas_call(
        project_kernel,
        out_shape=jax.ShapeDtypeStruct((groups, count, rows, cols), jnp.bfloat16),
        in_specs=[pl.BlockSpec(memory_space=pltpu.SMEM)] + [vmem] * (1 + count),
        out_specs=vmem,
        compiler_params=pltpu.CompilerParams(vmem_limit_bytes=12 * 2**20),
        name="project",
    )(place, attended, *weights)


def swap(x, axis):
    return lax.all_to_all(x, axis, 0, 0, tiled=True)


def total_of(parts):
    return functools.reduce(
        jnp.add, [parts[i].astype(jnp.float32) for i in range(parts.shape[0])]
    ).astype(jnp.bfloat16)


def copies(x, count):
    return jnp.broadcast_to(x[None], (count, *x.shape))


def on_device(text_states, w_query, w_out, visual_keys, visual_values, block_list):
    vis, hs = ("z", "y"), ("head", "sec")
    nz, ny, groups = (lax.axis_size(a) for a in ("z", "y", hs))
    weights = [w_out] + [
        lax.ppermute(w_out, "y", [(i, (i + d) % ny) for i in range(ny)])
        for d in range(1, ny)
    ]
    terms = jnp.dot(text_states, w_query, preferred_element_type=jnp.float32)
    terms = terms.astype(jnp.bfloat16)
    terms = total_of(swap(terms.reshape(nz * ny, -1, terms.shape[1]), ("y", "z")))
    query = swap(copies(terms, nz * ny), ("y", "z")).reshape(-1, terms.shape[1])
    ids = block_list[:, 0, :]
    partial = attention(ids, query, visual_keys, visual_values)
    parts = swap(partial.reshape(nz * ny, -1, partial.shape[1]), vis)
    attended = swap(merge(parts, nz), "z")
    out = project(attended.reshape(-1, attended.shape[-1]), weights, groups, "y")
    parts = swap(out.reshape(groups * ny, *out.shape[2:]), (*hs, "y")).reshape(out.shape)
    return total_of(parts).reshape(-1, out.shape[-1])


def solution(mesh):
    heads, vis, sec = (mesh.shape[a] for a in ("head", "vis", "sec"))
    ny = 4 if vis % 4 == 0 and vis > 4 else 2
    fine = Mesh(mesh.devices.reshape(heads, ny, vis // ny, sec), ("head", "y", "z", "sec"))
    vy, hs = ("y", "z"), ("head", "sec")
    in_specs = (
        P(None, vy),
        P(vy, hs),
        P(hs, vy),
        P(vy, hs),
        P(vy, hs),
        P(None, vy, None),
    )
    return jax.shard_map(
        on_device, mesh=fine, in_specs=in_specs, out_specs=P(hs, vy), check_vma=False
    )
```

profile of v0, /device:TPU:1, one launch (start us, length us, event | category | flops | bytes accessed | tf_op | source)
XLA Modules:
  0.0 121.1 jit_solution(8084985179202785927)
XLA Ops:
  0.0 0.0 copy-start
  0.0 0.0 copy-start.4
  0.0 0.0 copy-start.2
  0.0 0.0 copy-start.1
  0.0 1.0 copy-done
  1.0 1.6 %fusion = bf16[32,8,1024]{2,1,0:T(8,128)(2,1)S(1)} fusion(bf16[256,256]{1,0:T(8,128)(2,1)} %param.6, bf16[256,1024]{1,0:T(8,128)(2,1)S(1)} %copy-done), kind=kOutput, calls=%fused_computation.1 | convolution fusion | flops 134479872 | bytes 1179648 | tf_op jit(solution)/shard_map/dot_general | solution.py:230
  2.6 26.4 %all_to_all.25 = bf16[32,8,1024]{2,1,0:T(8,128)(2,1)S(1)} all-to-all(bf16[32,8,1024]{2,1,0:T(8,128)(2,1)S(1)} %fusion), channel_id=1, replica_groups=mesh['head'=4,'y'=4,'z'=8,'sec'=2] {'y','z'}, dimensions={0} | all-to-all | bytes 1048576 | tf_op jit(solution)/shard_map/all_to_all | solution.py:210
  29.0 0.1 fusion.2
  29.1 0.1 broadcast_in_dim.9
  29.1 20.9 %all_to_all.26 = bf16[32,8,1024]{2,1,0:T(8,128)(2,1)S(1)} all-to-all(bf16[32,8,1024]{2,1,0:T(8,128)(2,1)S(1)} %broadcast_in_dim.9), channel_id=1, replica_groups=mesh['head'=4,'y'=4,'z'=8,'sec'=2] {'y','z'}, dimensions={0} | all-to-all | bytes 1048576 | tf_op jit(solution)/shard_map/all_to_all | solution.py:210
  50.0 0.0 copy-done.4
  50.0 0.0 copy-done.2
  50.0 0.0 copy-done.1
  50.0 0.0 copy-start.3
  50.0 12.0 %attend.1 = bf16[256,1152]{1,0:T(8,128)(2,1)} custom-call(s32[2,32]{1,0:T(2,128)S(1)} %bitcast.17, bf16[256,1024]{1,0:T(8,128)(2,1)S(1)} %bitcast.14, bf16[8192,128]{1,0:T(8,128)(2,1)S(1)} %copy-done.1, bf16[8192,128]{1,0:T(8,128)(2,1)S(1)} %copy-done.2), custom_call_target="tpu_custom_call" | custom-call | tf_op jit(solution)/shard_map/attend/pallas_call | solution.py:128
  62.0 10.7 %all-to-all-start.2 = ((bf16[32,8,1152]{2,1,0:T(8,128)(2,1)}), bf16[32,8,1152]{2,1,0:T(8,128)(2,1)S(1)}, u32[]{:S(2)}, u32[]{:S(2)}) async-start(bf16[32,8,1152]{2,1,0:T(8,128)(2,1)} %bitcast.5), calls=%async_computation.2 | async-start | bytes 1179648 | tf_op jit(solution)/shard_map/all_to_all | solution.py:210
  72.7 0.0 copy-done.3
  72.7 2.8 %collective-permute-start.1 = (bf16[1024,256]{1,0:T(8,128)(2,1)S(1)}, bf16[1024,256]{1,0:T(8,128)(2,1)S(1)}, u32[]{:S(2)}, u32[]{:S(2)}) collective-permute-start(bf16[1024,256]{1,0:T(8,128)(2,1)S(1)} %copy-done.3), channel_id=1, source_target_pairs={{0,32},{16,48},{32,0},{48,16},{1,33},{17,49},{33,1},{49,17},{2,34}... | collective-permute-start | bytes 1572872 | tf_op jit(solution)/shard_map/ppermute | solution.py:227
  75.6 0.3 collective-permute-start
  75.8 2.4 %collective-permute-start.2 = (bf16[1024,256]{1,0:T(8,128)(2,1)S(1)}, bf16[1024,256]{1,0:T(8,128)(2,1)S(1)}, u32[]{:S(2)}, u32[]{:S(2)}) collective-permute-start(bf16[1024,256]{1,0:T(8,128)(2,1)S(1)} %copy-done.3), channel_id=1, source_target_pairs={{0,48},{16,0},{32,16},{48,32},{1,49},{17,1},{33,17},{49,33},{2,50}... | collective-permute-start | bytes 1572872 | tf_op jit(solution)/shard_map/ppermute | solution.py:227
  78.2 12.0 %all-to-all-done.2.parts_ref = bf16[32,8,1152]{2,1,0:T(8,128)(2,1)S(1)} async-done(((bf16[32,8,1152]{2,1,0:T(8,128)(2,1)}), bf16[32,8,1152]{2,1,0:T(8,128)(2,1)S(1)}, u32[]{:S(2)}, u32[]{:S(2)}) %all-to-all-start.2) | async-done | bytes 589856 | tf_op jit(solution)/shard_map/all_to_all | solution.py:210
  90.2 1.1 merge.1
  91.4 3.4 %all-to-all-start.3 = ((bf16[8,8,1024]{2,1,0:T(8,128)(2,1)}), bf16[8,8,1024]{2,1,0:T(8,128)(2,1)S(1)}, u32[]{:S(2)}, u32[]{:S(2)}) async-start(bf16[8,8,1024]{2,1,0:T(8,128)(2,1)} %merge.1), calls=%async_computation.3 | async-start | bytes 262144 | tf_op jit(solution)/shard_map/all_to_all | solution.py:210
  94.7 0.0 collective-permute-done.1.refs_2_
  94.7 10.9 %collective-permute-done.refs_1_ = bf16[1024,256]{1,0:T(8,128)(2,1)S(1)} collective-permute-done((bf16[1024,256]{1,0:T(8,128)(2,1)S(1)}, bf16[1024,256]{1,0:T(8,128)(2,1)S(1)}, u32[]{:S(2)}, u32[]{:S(2)}) %collective-permute-start) | collective-permute-done | bytes 524320 | tf_op jit(solution)/shard_map/ppermute | solution.py:227
  105.7 0.0 collective-permute-done.2.refs_3_
  105.7 0.0 all-to-all-done.3
  105.7 0.5 project.1
  106.2 14.3 %all_to_all.27 = bf16[32,8,256]{2,1,0:T(8,128)(2,1)S(1)} all-to-all(bf16[32,8,256]{2,1,0:T(8,128)(2,1)S(1)} %bitcast.16), channel_id=1, replica_groups=mesh['head'=4,'y'=4,'z'=8,'sec'=2] {'head','sec','y'}, dimensions={0} | all-to-all | bytes 262144 | tf_op jit(solution)/shard_map/all_to_all | solution.py:210
  120.5 0.6 fusion.1
Async XLA Ops:
  0.0 1.0 copy-start
  0.0 50.0 %copy-start.4 = (s32[2,1,32]{2,1,0:T(1,128)S(1)}, s32[2,1,32]{2,1,0:T(1,128)}, u32[]{:S(2)}) copy-start(s32[2,1,32]{2,1,0:T(1,128)} %param.11) | copy-start | bytes 772
  0.0 50.0 %copy-start.2 = (bf16[8192,128]{1,0:T(8,128)(2,1)S(1)}, bf16[8192,128]{1,0:T(8,128)(2,1)}, u32[]{:S(2)}) copy-start(bf16[8192,128]{1,0:T(8,128)(2,1)} %v_ref.1) | copy-start | bytes 6291460
  0.0 50.0 %copy-start.1 = (bf16[8192,128]{1,0:T(8,128)(2,1)S(1)}, bf16[8192,128]{1,0:T(8,128)(2,1)}, u32[]{:S(2)}) copy-start(bf16[8192,128]{1,0:T(8,128)(2,1)} %k_ref.1) | copy-start | bytes 6291460
  50.0 22.7 %copy-start.3 = (bf16[1024,256]{1,0:T(8,128)(2,1)S(1)}, bf16[1024,256]{1,0:T(8,128)(2,1)}, u32[]{:S(2)}) copy-start(bf16[1024,256]{1,0:T(8,128)(2,1)} %refs_0_.1) | copy-start | bytes 1572868
  62.0 28.2 %all-to-all-start.2 = ((bf16[32,8,1152]{2,1,0:T(8,128)(2,1)}), bf16[32,8,1152]{2,1,0:T(8,128)(2,1)S(1)}, u32[]{:S(2)}, u32[]{:S(2)}) async-start(bf16[32,8,1152]{2,1,0:T(8,128)(2,1)} %bitcast.5), calls=%async_computation.2 | async-start | bytes 1179648 | tf_op jit(solution)/shard_map/all_to_all | solution.py:210
  72.7 22.0 %collective-permute-start.1 = (bf16[1024,256]{1,0:T(8,128)(2,1)S(1)}, bf16[1024,256]{1,0:T(8,128)(2,1)S(1)}, u32[]{:S(2)}, u32[]{:S(2)}) collective-permute-start(bf16[1024,256]{1,0:T(8,128)(2,1)S(1)} %copy-done.3), channel_id=1, source_target_pairs={{0,32},{16,48},{32,0},{48,16},{1,33},{17,49},{33,1},{49,17},{2,34}... | collective-permute-start | bytes 1572872 | tf_op jit(solution)/shard_map/ppermute | solution.py:227
  75.6 30.1 %collective-permute-start = (bf16[1024,256]{1,0:T(8,128)(2,1)S(1)}, bf16[1024,256]{1,0:T(8,128)(2,1)S(1)}, u32[]{:S(2)}, u32[]{:S(2)}) collective-permute-start(bf16[1024,256]{1,0:T(8,128)(2,1)S(1)} %copy-done.3), channel_id=1, source_target_pairs={{0,16},{16,32},{32,48},{48,0},{1,17},{17,33},{33,49},{49,1},{2,18}... | collective-permute-start | bytes 1572872 | tf_op jit(solution)/shard_map/ppermute | solution.py:227
  75.8 29.8 %collective-permute-start.2 = (bf16[1024,256]{1,0:T(8,128)(2,1)S(1)}, bf16[1024,256]{1,0:T(8,128)(2,1)S(1)}, u32[]{:S(2)}, u32[]{:S(2)}) collective-permute-start(bf16[1024,256]{1,0:T(8,128)(2,1)S(1)} %copy-done.3), channel_id=1, source_target_pairs={{0,48},{16,0},{32,16},{48,32},{1,49},{17,1},{33,17},{49,33},{2,50}... | collective-permute-start | bytes 1572872 | tf_op jit(solution)/shard_map/ppermute | solution.py:227
  91.4 14.3 %all-to-all-start.3 = ((bf16[8,8,1024]{2,1,0:T(8,128)(2,1)}), bf16[8,8,1024]{2,1,0:T(8,128)(2,1)S(1)}, u32[]{:S(2)}, u32[]{:S(2)}) async-start(bf16[8,8,1024]{2,1,0:T(8,128)(2,1)} %merge.1), calls=%async_computation.3 | async-start | bytes 262144 | tf_op jit(solution)/shard_map/all_to_all | solution.py:210
where the time goes:
time: 122 us; the launch traced here: 121 us
  blocking collectives  61.5 us (50%)
  waiting for transfers between devices  23 us (19%)
  starting transfers between devices  19.5 us (16%)
  Pallas kernels  13.6 us (11%)
  matrix products  1.6 us (1%)
    all_to_all x3, blocking collectives, swap(): return lax.all_to_all(x, axis, 0, 0, tiled=True)  61.5 us
    all_to_all x2, starting transfers between devices, swap(): return lax.all_to_all(x, axis, 0, 0, tiled=True)  14 us
    pallas_call x1, Pallas kernels, attention(): pl.pallas_call(functools.partial(attention_kernel, heads), out_shape=jax....  12 us
    all_to_all x2, waiting for transfers between devices, swap(): return lax.all_to_all(x, axis, 0, 0, tiled=True)  12 us
    ppermute x3, waiting for transfers between devices, on_device(): lax.ppermute(w_out, 'y', [(i, (i + d) % ny) for i in range(ny)])  10.9 us
    ppermute x3, starting transfers between devices, on_device(): lax.ppermute(w_out, 'y', [(i, (i + d) % ny) for i in range(ny)])  5.5 us
  transfers between devices with their start and end apart: 5, of which 2 were waited for; matrix products, arithmetic and copies ran while one was open for 0% of the time, Pallas kernels for 1%

commit v1 on v0

--- a/solution.py
+++ b/solution.py
@@ -179,27 +179,29 @@
 
 
 def project_kernel(place_ref, attended_ref, *refs):
-    w_refs, out_ref = refs[:-1], refs[-1]
-    count = len(w_refs)
+    near, right, far_top, far_low, left, out_ref = refs
+    half, count = far_top.shape[0], out_ref.shape[1]
     groups, _, rows, _ = out_ref.shape
     attended = attended_ref[...]
-    for k, w_ref in enumerate(w_refs):
+    whole = lambda w_ref: jnp.dot(attended, w_ref[...], preferred_element_type=jnp.float32)
+    halves = jnp.dot(attended[:, :half], far_top[...], preferred_element_type=jnp.float32)
+    halves = halves + jnp.dot(attended[:, half:], far_low[...], preferred_element_type=jnp.float32)
+    for k, out in enumerate((whole(near), whole(right), halves, whole(left))):
         place = lax.rem(place_ref[0] + (count - k), count)
-        out = jnp.dot(attended, w_ref[...], preferred_element_type=jnp.float32)
         out = out.astype(jnp.bfloat16)
         for g in range(groups):
             out_ref[g, place] = out[g * rows : (g + 1) * rows]
 
 
 def project(attended, weights, groups, axis):
-    count = len(weights)
+    count = lax.axis_size(axis)
     vmem = pl.BlockSpec(memory_space=pltpu.VMEM)
     place = jnp.reshape(lax.axis_index(axis), (1,)).astype(jnp.int32)
     rows, cols = attended.shape[0] // groups, weights[0].shape[1]
     return pl.pallas_call(
         project_kernel,
         out_shape=jax.ShapeDtypeStruct((groups, count, rows, cols), jnp.bfloat16),
-        in_specs=[pl.BlockSpec(memory_space=pltpu.SMEM)] + [vmem] * (1 + count),
+        in_specs=[pl.BlockSpec(memory_space=pltpu.SMEM)] + [vmem] * (1 + len(weights)),
         out_specs=vmem,
         compiler_params=pltpu.CompilerParams(vmem_limit_bytes=12 * 2**20),
         name="project",
@@ -223,14 +225,15 @@
 def on_device(text_states, w_query, w_out, visual_keys, visual_values, block_list):
     vis, hs = ("z", "y"), ("head", "sec")
     nz, ny, groups = (lax.axis_size(a) for a in ("z", "y", hs))
-    weights = [w_out] + [
-        lax.ppermute(w_out, "y", [(i, (i + d) % ny) for i in range(ny)])
-        for d in range(1, ny)
-    ]
+    shift = lambda x, d: lax.ppermute(x, "y", [(i, (i + d) % ny) for i in range(ny)])
+    half = w_out.shape[0] // 2
+    right, left = shift(w_out, 1), shift(w_out, 3)
+    weights = [w_out, right, shift(w_out[:half], 2), shift(left[half:], 3), left]
     terms = jnp.dot(text_states, w_query, preferred_element_type=jnp.float32)
     terms = terms.astype(jnp.bfloat16)
     terms = total_of(swap(terms.reshape(nz * ny, -1, terms.shape[1]), ("y", "z")))
-    query = swap(copies(terms, nz * ny), ("y", "z")).reshape(-1, terms.shape[1])
+    mine = swap(copies(terms, nz), "z").reshape(-1, terms.shape[1])
+    query = swap(copies(mine, ny), "y").reshape(-1, terms.shape[1])
     ids = block_list[:, 0, :]
     partial = attention(ids, query, visual_keys, visual_values)
     parts = swap(partial.reshape(nz * ny, -1, partial.shape[1]), vis)

time: 122 us -> 128 us (1.049)
  blocking collectives: 61.5 us -> 68 us
    all_to_all x3 -> x4, blocking collectives: 61.5 us -> 68 us  [swap(): return lax.all_to_all(x, axis, 0, 0, tiled=True)]
    all_to_all x2, waiting for transfers between devices: 12 us -> 7.9 us  [swap(): return lax.all_to_all(x, axis, 0, 0, tiled=True)]
    ppermute x3 -> x4, waiting for transfers between devices: 10.9 us -> 15 us  [on_device(): lax.ppermute(x, 'y', [(i, (i + d) % ny) for i in range(ny)])]
    all_to_all x2, starting transfers between devices: 14 us -> 10.1 us  [swap(): return lax.all_to_all(x, axis, 0, 0, tiled=True)]
    ppermute x3 -> x4, starting transfers between devices: 5.5 us -> 8.27 us  [on_device(): lax.ppermute(x, 'y', [(i, (i + d) % ny) for i in range(ny)])]
  transfers between devices with their start and end apart: 5 -> 6, of which waited for: 2 -> 2; matrix products, arithmetic and copies ran while one was open for 0% -> 1% of each run, Pallas kernels for 1% -> 1%
where the time goes in v1:
time: 128 us; the launch traced here: 127 us
  blocking collectives  68 us (53%)
  waiting for transfers between devices  22.9 us (18%)
  starting transfers between devices  18.4 us (14%)
  Pallas kernels  13.6 us (11%)
  local copies, waits for them, and re-layouts  1.87 us (1%)
  matrix products  1.35 us (1%)
    all_to_all x4, blocking collectives, swap(): return lax.all_to_all(x, axis, 0, 0, tiled=True)  68 us
    ppermute x4, waiting for transfers between devices, on_device(): lax.ppermute(x, 'y', [(i, (i + d) % ny) for i in range(ny)])  15 us
    pallas_call x1, Pallas kernels, attention(): pl.pallas_call(functools.partial(attention_kernel, heads), out_shape=jax....  12 us
    all_to_all x2, starting transfers between devices, swap(): return lax.all_to_all(x, axis, 0, 0, tiled=True)  10.1 us
    ppermute x4, starting transfers between devices, on_device(): lax.ppermute(x, 'y', [(i, (i + d) % ny) for i in range(ny)])  8.27 us
    all_to_all x2, waiting for transfers between devices, swap(): return lax.all_to_all(x, axis, 0, 0, tiled=True)  7.9 us
  transfers between devices with their start and end apart: 6, of which 2 were waited for; matrix products, arithmetic and copies ran while one was open for 1% of the time, Pallas kernels for 1%

profile of v1, /device:TPU:1, one launch (start us, length us, event | category | flops | bytes accessed | tf_op | source)
XLA Modules:
  0.0 127.0 jit_solution(11724429167603075032)
XLA Ops:
  0.0 0.0 copy-start
  0.0 1.0 copy-done
  1.0 0.0 copy-start.2
  1.0 1.4 %fusion = bf16[32,8,1024]{2,1,0:T(8,128)(2,1)S(1)} fusion(bf16[256,256]{1,0:T(8,128)(2,1)} %param.6, bf16[256,1024]{1,0:T(8,128)(2,1)S(1)} %copy-done), kind=kOutput, calls=%fused_computation.1 | convolution fusion | flops 134479872 | bytes 1179648 | tf_op jit(solution)/shard_map/dot_general | solution.py:232
  2.4 0.0 copy-start.1
  2.4 0.0 copy-start.4
  2.4 26.5 %all_to_all.30 = bf16[32,8,1024]{2,1,0:T(8,128)(2,1)S(1)} all-to-all(bf16[32,8,1024]{2,1,0:T(8,128)(2,1)S(1)} %fusion), channel_id=1, replica_groups=mesh['head'=4,'y'=4,'z'=8,'sec'=2] {'y','z'}, dimensions={0} | all-to-all | bytes 1048576 | tf_op jit(solution)/shard_map/all_to_all | solution.py:212
  28.9 0.1 fusion.2
  29.0 13.1 %all_to_all.31 = bf16[8,8,1024]{2,1,0:T(8,128)(2,1)S(1)} all-to-all(bf16[8,8,1024]{2,1,0:T(8,128)(2,1)S(1)} %broadcast_in_dim.16), channel_id=1, replica_groups=mesh['head'=4,'y'=4,'z'=8,'sec'=2] {'z'}, dimensions={0} | all-to-all | bytes 262144 | tf_op jit(solution)/shard_map/all_to_all | solution.py:212
  42.2 9.8 %all_to_all.32 = bf16[4,64,1024]{2,1,0:T(8,128)(2,1)S(1)} all-to-all(bf16[4,64,1024]{2,1,0:T(8,128)(2,1)S(1)} %broadcast_in_dim.18), channel_id=1, replica_groups=mesh['head'=4,'y'=4,'z'=8,'sec'=2] {'y'}, dimensions={0} | all-to-all | bytes 1048576 | tf_op jit(solution)/shard_map/all_to_all | solution.py:212
  52.0 0.0 copy-done.2
  52.0 0.0 copy-done.1
  52.0 0.0 copy-done.4
  52.0 0.0 copy-start.3
  52.0 12.0 %attend.1 = bf16[256,1152]{1,0:T(8,128)(2,1)} custom-call(s32[2,32]{1,0:T(2,128)S(1)} %bitcast.18, bf16[256,1024]{1,0:T(8,128)(2,1)S(1)} %bitcast.15, bf16[8192,128]{1,0:T(8,128)(2,1)S(1)} %copy-done.1, bf16[8192,128]{1,0:T(8,128)(2,1)S(1)} %copy-done.2), custom_call_target="tpu_custom_call" | custom-call | tf_op jit(solution)/shard_map/attend/pallas_call | solution.py:128
  64.0 5.3 %all-to-all-start.3 = ((bf16[32,8,1152]{2,1,0:T(8,128)(2,1)}), bf16[32,8,1152]{2,1,0:T(8,128)(2,1)S(1)}, u32[]{:S(2)}, u32[]{:S(2)}) async-start(bf16[32,8,1152]{2,1,0:T(8,128)(2,1)} %bitcast.6), calls=%async_computation.3 | async-start | bytes 1179648 | tf_op jit(solution)/shard_map/all_to_all | solution.py:212
  69.3 0.0 copy-done.3
  69.3 2.5 %collective-permute-start.2 = (bf16[1024,256]{1,0:T(8,128)(2,1)S(1)}, bf16[1024,256]{1,0:T(8,128)(2,1)S(1)}, u32[]{:S(2)}, u32[]{:S(2)}) collective-permute-start(bf16[1024,256]{1,0:T(8,128)(2,1)S(1)} %copy-done.3), channel_id=1, source_target_pairs={{0,48},{16,0},{32,16},{48,32},{1,49},{17,1},{33,17},{49,33},{2,50}... | collective-permute-start | bytes 1572872 | tf_op jit(solution)/shard_map/ppermute | solution.py:228
  71.8 0.0 collective-permute-start
  71.9 1.8 %collective-permute-start.1 = (bf16[512,256]{1,0:T(8,128)(2,1)S(1)}, bf16[512,256]{1,0:T(8,128)(2,1)S(1)}, u32[]{:S(2)}, u32[]{:S(2)}) collective-permute-start(bf16[512,256]{1,0:T(8,128)(2,1)S(1)} %slice.166), channel_id=1, source_target_pairs={{0,32},{16,48},{32,0},{48,16},{1,33},{17,49},{33,1},{49,17},{2,34}... | collective-permute-start | bytes 786440 | tf_op jit(solution)/shard_map/ppermute | solution.py:228
  73.7 15.0 %collective-permute-done.2.refs_4_ = bf16[1024,256]{1,0:T(8,128)(2,1)S(1)} collective-permute-done((bf16[1024,256]{1,0:T(8,128)(2,1)S(1)}, bf16[1024,256]{1,0:T(8,128)(2,1)S(1)}, u32[]{:S(2)}, u32[]{:S(2)}) %collective-permute-start.2) | collective-permute-done | bytes 524320 | tf_op jit(solution)/shard_map/ppermute | solution.py:228
  88.7 0.7 slice.208
  89.4 3.9 %collective-permute-start.3 = (bf16[512,256]{1,0:T(8,128)(2,1)}, bf16[512,256]{1,0:T(8,128)(2,1)S(1)}, u32[]{:S(2)}, u32[]{:S(2)}) collective-permute-start(bf16[512,256]{1,0:T(8,128)(2,1)} %slice.208), channel_id=1, source_target_pairs={{0,48},{16,0},{32,16},{48,32},{1,49},{17,1},{33,17},{49,33},{2,50}... | collective-permute-start | bytes 786440 | tf_op jit(solution)/shard_map/ppermute | solution.py:228
  93.3 0.0 all-to-all-done.3.parts_ref
  93.3 1.1 merge.1
  94.4 4.9 %all-to-all-start.4 = ((bf16[8,8,1024]{2,1,0:T(8,128)(2,1)}), bf16[8,8,1024]{2,1,0:T(8,128)(2,1)S(1)}, u32[]{:S(2)}, u32[]{:S(2)}) async-start(bf16[8,8,1024]{2,1,0:T(8,128)(2,1)} %merge.1), calls=%async_computation.4 | async-start | bytes 262144 | tf_op jit(solution)/shard_map/all_to_all | solution.py:212
  99.3 0.0 collective-permute-done.1.refs_2_
  99.3 0.0 collective-permute-done.refs_1_
  99.3 0.0 collective-permute-done.3.refs_3_
  99.4 7.9 %all-to-all-done.4 = bf16[8,8,1024]{2,1,0:T(8,128)(2,1)S(1)} async-done(((bf16[8,8,1024]{2,1,0:T(8,128)(2,1)}), bf16[8,8,1024]{2,1,0:T(8,128)(2,1)S(1)}, u32[]{:S(2)}, u32[]{:S(2)}) %all-to-all-start.4) | async-done | bytes 131104 | tf_op jit(solution)/shard_map/all_to_all | solution.py:212
  107.3 0.5 project.1
  107.7 18.7 %all_to_all.33 = bf16[32,8,256]{2,1,0:T(8,128)(2,1)S(1)} all-to-all(bf16[32,8,256]{2,1,0:T(8,128)(2,1)S(1)} %bitcast.17), channel_id=1, replica_groups=mesh['head'=4,'y'=4,'z'=8,'sec'=2] {'head','sec','y'}, dimensions={0} | all-to-all | bytes 262144 | tf_op jit(solution)/shard_map/all_to_all | solution.py:212
  126.4 0.6 fusion.1
  (3 shorter events, 0.1 us)
Async XLA Ops:
  0.0 1.0 copy-start
  1.0 50.9 %copy-start.2 = (bf16[8192,128]{1,0:T(8,128)(2,1)S(1)}, bf16[8192,128]{1,0:T(8,128)(2,1)}, u32[]{:S(2)}) copy-start(bf16[8192,128]{1,0:T(8,128)(2,1)} %v_ref.1) | copy-start | bytes 6291460
  2.4 49.6 %copy-start.1 = (bf16[8192,128]{1,0:T(8,128)(2,1)S(1)}, bf16[8192,128]{1,0:T(8,128)(2,1)}, u32[]{:S(2)}) copy-start(bf16[8192,128]{1,0:T(8,128)(2,1)} %k_ref.1) | copy-start | bytes 6291460
  2.4 49.6 %copy-start.4 = (s32[2,1,32]{2,1,0:T(1,128)S(1)}, s32[2,1,32]{2,1,0:T(1,128)}, u32[]{:S(2)}) copy-start(s32[2,1,32]{2,1,0:T(1,128)} %param.11) | copy-start | bytes 772
  52.0 17.3 %copy-start.3 = (bf16[1024,256]{1,0:T(8,128)(2,1)S(1)}, bf16[1024,256]{1,0:T(8,128)(2,1)}, u32[]{:S(2)}) copy-start(bf16[1024,256]{1,0:T(8,128)(2,1)} %refs_0_.1) | copy-start | bytes 1572868
  64.0 29.3 %all-to-all-start.3 = ((bf16[32,8,1152]{2,1,0:T(8,128)(2,1)}), bf16[32,8,1152]{2,1,0:T(8,128)(2,1)S(1)}, u32[]{:S(2)}, u32[]{:S(2)}) async-start(bf16[32,8,1152]{2,1,0:T(8,128)(2,1)} %bitcast.6), calls=%async_computation.3 | async-start | bytes 1179648 | tf_op jit(solution)/shard_map/all_to_all | solution.py:212
  69.3 19.4 %collective-permute-start.2 = (bf16[1024,256]{1,0:T(8,128)(2,1)S(1)}, bf16[1024,256]{1,0:T(8,128)(2,1)S(1)}, u32[]{:S(2)}, u32[]{:S(2)}) collective-permute-start(bf16[1024,256]{1,0:T(8,128)(2,1)S(1)} %copy-done.3), channel_id=1, source_target_pairs={{0,48},{16,0},{32,16},{48,32},{1,49},{17,1},{33,17},{49,33},{2,50}... | collective-permute-start | bytes 1572872 | tf_op jit(solution)/shard_map/ppermute | solution.py:228
  71.8 27.5 %collective-permute-start = (bf16[1024,256]{1,0:T(8,128)(2,1)S(1)}, bf16[1024,256]{1,0:T(8,128)(2,1)S(1)}, u32[]{:S(2)}, u32[]{:S(2)}) collective-permute-start(bf16[1024,256]{1,0:T(8,128)(2,1)S(1)} %copy-done.3), channel_id=1, source_target_pairs={{0,16},{16,32},{32,48},{48,0},{1,17},{17,33},{33,49},{49,1},{2,18}... | collective-permute-start | bytes 1572872 | tf_op jit(solution)/shard_map/ppermute | solution.py:228
  71.9 27.5 %collective-permute-start.1 = (bf16[512,256]{1,0:T(8,128)(2,1)S(1)}, bf16[512,256]{1,0:T(8,128)(2,1)S(1)}, u32[]{:S(2)}, u32[]{:S(2)}) collective-permute-start(bf16[512,256]{1,0:T(8,128)(2,1)S(1)} %slice.166), channel_id=1, source_target_pairs={{0,32},{16,48},{32,0},{48,16},{1,33},{17,49},{33,1},{49,17},{2,34}... | collective-permute-start | bytes 786440 | tf_op jit(solution)/shard_map/ppermute | solution.py:228
  89.4 9.9 %collective-permute-start.3 = (bf16[512,256]{1,0:T(8,128)(2,1)}, bf16[512,256]{1,0:T(8,128)(2,1)S(1)}, u32[]{:S(2)}, u32[]{:S(2)}) collective-permute-start(bf16[512,256]{1,0:T(8,128)(2,1)} %slice.208), channel_id=1, source_target_pairs={{0,48},{16,0},{32,16},{48,32},{1,49},{17,1},{33,17},{49,33},{2,50}... | collective-permute-start | bytes 786440 | tf_op jit(solution)/shard_map/ppermute | solution.py:228
  94.4 12.8 %all-to-all-start.4 = ((bf16[8,8,1024]{2,1,0:T(8,128)(2,1)}), bf16[8,8,1024]{2,1,0:T(8,128)(2,1)S(1)}, u32[]{:S(2)}, u32[]{:S(2)}) async-start(bf16[8,8,1024]{2,1,0:T(8,128)(2,1)} %merge.1), calls=%async_computation.4 | async-start | bytes 262144 | tf_op jit(solution)/shard_map/all_to_all | solution.py:212
